TPU v7x, 32 devices: a whole 2x2x4 slice. The times are simulated.
32 devices in a mesh: dp: 16 (over z, y, core), rows: 2 (over x).
Axes of the slice: x: 2, y: 2, z: 4, core: 2. Of those that a mesh axis runs over, the one named last changes fastest.
Arguments:
- latents: bfloat16 [16, 4, 128, 320], P('dp', 'rows'), may hold values from -6 to 6
- mean_one: float32 [16, 32], P('dp'), may hold values from -0.5 to 0.5
- rstd_one: float32 [16, 32], P('dp'), may hold values from 0.5 to 2
- gain_one: float32 [320], replicated, may hold values from 0.25 to 1.75
- shift_one: float32 [320], replicated, may hold values from -0.5 to 0.5
- kernel_one: bfloat16 [4, 9, 25600], P(None, None, 'dp'), may hold values from -0.109375 to 0.109375
- bias_one: float32 [320], replicated, may hold values from -3 to 3
- embed_bias: float32 [16, 320], P('dp'), may hold values from -3 to 3
- mean_two: float32 [16, 32], P('dp'), may hold values from -0.5 to 0.5
- rstd_two: float32 [16, 32], P('dp'), may hold values from 0.5 to 2
- gain_two: float32 [320], replicated, may hold values from 0.25 to 1.75
- shift_two: float32 [320], replicated, may hold values from -0.5 to 0.5
- kernel_two: bfloat16 [4, 9, 25600], P(None, None, 'dp'), may hold values from -0.109375 to 0.109375
- bias_two: float32 [320], replicated, may hold values from -3 to 3
Outputs:
- block_out: bfloat16 [16, 4, 128, 320], P('dp', 'rows')
All inputs are finite; a program needn't handle non-finite values.
Results may differ from a plain program's by a relative error of at most 0.0045.
Values may be sent and summed in bfloat16 or wider, within the bound.
No kernel may reach another device: no remote copies, remote signals or barrier semaphores. Data moves between devices by JAX's collectives and lax.ppermute only.
A program may use at most 192 MiB of HBM per device.

v0:
```python
import jax
import jax.numpy as jnp
from jax import lax
from jax.sharding import PartitionSpec as P


def padded_2(array, sides, width):
    for axis, dim in sides:
        devices, length = (lax.axis_size(axis), array.shape[dim])
        up = [(i, (i + 1) % devices) for i in range(devices - 1)]
        down = [(j, i) for i, j in up]
        last = lax.slice_in_dim(array, length - width, length, axis=dim)
        first = lax.slice_in_dim(array, 0, width, axis=dim)
        before = lax.ppermute(last, axis, up)
        after = lax.ppermute(first, axis, down)
        array = jnp.concatenate([before, array, after], axis=dim)
    return array


def norm_silu(values, group_mean, group_rstd, gain_vec, shift_vec):
    height, columns, channels = values.shape
    groups = group_mean.shape[-1]
    grouped = values.reshape(height, columns, groups, channels // groups)
    scaled = (grouped - group_mean[0][:, None]) * group_rstd[0][:, None]
    return jax.nn.silu(scaled.reshape(height, columns, channels) * gain_vec + shift_vec)


def padded_rows(activation):
    padded = padded_2(activation, (("rows", 0),), 1)
    return jnp.pad(padded, ((0, 0), (1, 1), (0, 0)))


def window_at(padded, position, height, columns, first_channel, depth):
    tap_row = position // 3
    tap_col = position % 3
    window = padded[
        tap_row : tap_row + height,
        tap_col : tap_col + columns,
        first_channel : first_channel + depth,
    ]
    return window.reshape(height * columns, depth)


def reorder_whole(whole_kernel, channels):
    blocks = whole_kernel.shape[0]
    split = whole_kernel.reshape(blocks, 9, channels // blocks, channels)
    return jnp.transpose(split, (1, 0, 2, 3)).reshape(3, 3 * channels, channels)


def whole_weights(kernel, channels):
    whole_kernel = lax.all_gather(kernel, "dp", axis=2, tiled=True)
    return reorder_whole(whole_kernel, channels)


def convolve_whole(activation, weights):
    height, columns, channels = activation.shape
    padded = padded_rows(activation)
    accumulated = jnp.zeros((height * columns, channels), jnp.float32)
    for tap_row in range(3):
        windows = jnp.concatenate(
            [
                window_at(padded, 3 * tap_row + tap_col, height, columns, 0, channels)
                for tap_col in range(3)
            ],
            axis=1,
        )
        accumulated = accumulated + jnp.dot(
            windows, weights[tap_row], preferred_element_type=jnp.float32
        )
    return accumulated.reshape(height, columns, channels)


def shards(
    latents,
    mean_one,
    rstd_one,
    gain_one,
    shift_one,
    kernel_one,
    bias_one,
    embed_bias,
    mean_two,
    rstd_two,
    gain_two,
    shift_two,
    kernel_two,
    bias_two,
):
    channels = latents.shape[3]
    sample = latents[0].astype(jnp.float32)
    first_act = norm_silu(sample, mean_one, rstd_one, gain_one, shift_one).astype(jnp.bfloat16)
    hidden = (
        convolve_whole(first_act, whole_weights(kernel_one, channels)) + bias_one + embed_bias[0]
    )
    second_act = norm_silu(hidden, mean_two, rstd_two, gain_two, shift_two).astype(jnp.bfloat16)
    result = convolve_whole(second_act, whole_weights(kernel_two, channels)) + bias_two + sample
    return result.astype(jnp.bfloat16)[None]


def solution(mesh):
    placed = (
        P("dp", "rows", None, None),
        P("dp", None),
        P("dp", None),
        P(),
        P(),
        P(None, None, "dp"),
        P(),
        P("dp", None),
        P("dp", None),
        P("dp", None),
        P(),
        P(),
        P(None, None, "dp"),
        P(),
    )
    return jax.shard_map(
        shards, mesh=mesh, in_specs=placed, out_specs=P("dp", "rows", None, None), check_vma=False
    )
```

profile of v0, /device:TPU:0, one launch (start us, length us, event | category | flops | bytes accessed | tf_op | source)
XLA Modules:
  0.0 321.2 jit_solution(16401829512371649083)
XLA Ops:
  6.5 0.0 all-gather.3.cloned.1.call-start
  6.5 3.1 copy.65
  9.7 0.0 all-gather.3.cloned.1.call-update
  9.7 0.0 copy-start.11
  9.7 0.0 copy-start.12
  9.7 0.0 copy-start
  9.7 0.0 copy-start.4
  9.7 0.0 copy-start.5
  9.7 0.0 all-gather.5.cloned.1.call-start
  9.8 0.0 copy-done.3
  9.8 2.4 copy.77
  12.2 0.0 all-gather.5.cloned.1.call-update
  12.2 0.0 copy-start.10
  12.2 0.0 copy-done.11
  12.2 0.1 mul.80
  12.3 0.1 mul.81
  12.4 0.0 copy-done.12
  12.4 0.1 sub.41
  12.5 0.1 sub.42
  12.6 0.0 copy-done
  12.6 0.3 multiply_convert_fusion.3
  12.9 4.9 %collective-permute-start = (bf16[1,128,320]{1,2,0:T(8,128)(2,1)S(1)}, bf16[1,128,320]{1,2,0:T(8,128)(2,1)S(1)}, u32[]{:S(2)}, u32[]{:S(2)}) collective-permute-start(bf16[1,128,320]{1,2,0:T(8,128)(2,1)S(1)} %get-tuple-element.29), channel_id=1, source_target_pairs={{0,1},{2,3},{4,5},{6,7},{8,9},{10,11},{12,13},{14,15},{16,17},{18,... | collective-permute-start | bytes 245768 | tf_op jit(solution)/shard_map/ppermute | solution.py:14
  17.8 1.3 collective-permute-start.1
  19.1 0.2 copy.68
  19.3 0.9 multiply_convert_fusion.2
  20.2 0.1 mul.93
  20.3 0.1 mul.94
  20.4 0.0 copy-done.14
  20.4 0.1 sub.48
  20.4 0.1 sub.49
  20.6 0.0 collective-permute-done
  20.6 3.5 %collective-permute-done.1 = bf16[1,128,320]{1,2,0:T(8,128)(2,1)S(1)} collective-permute-done((bf16[1,128,320]{1,2,0:T(8,128)(2,1)S(1)}, bf16[1,128,320]{1,2,0:T(8,128)(2,1)S(1)}, u32[]{:S(2)}, u32[]{:S(2)}) %collective-permute-start.1) | collective-permute-done | bytes 81952 | tf_op jit(solution)/shard_map/ppermute | solution.py:15
  24.2 0.3 fusion.5
  24.5 0.2 slice_bitcast_fusion.7
  24.8 0.7 copy_bitcast_fusion.11
  25.5 120.5 %all-gather.3.cloned.1.call-done = bf16[4,9,25600]{1,0,2:T(4,128)(2,1)} async-done(((bf16[4,9,1600]{1,0,2:T(4,128)(2,1)}), bf16[4,9,25600]{1,0,2:T(4,128)(2,1)}) %all-gather.3.cloned.1.call-update) | async-done | bytes 1843216 | tf_op jit(solution)/shard_map/all_gather | solution.py:51
  146.0 30.0 %copy.66 = bf16[4,9,80,320]{3,2,0,1:T(8,128)(2,1)S(1)} copy(bf16[4,9,80,320]{1,0,3,2:T(4,128)(2,1)} %bitcast.136) | data formatting | bytes 3686400 | tf_op jit(solution)/shard_map/reshape | solution.py:46
  176.1 0.2 fusion.62
  176.3 0.0 copy-start.1
  176.3 0.4 fusion.6
  176.8 0.0 copy-start.6
  176.8 0.0 copy-start.7
  176.8 0.0 copy-start.8
  176.8 0.4 copy-done.1
  177.2 0.1 copy-done.2
  177.3 0.4 convolution_add_fusion.3
  177.8 0.6 multiply_convert_fusion
  178.4 0.3 multiply_convert_fusion.1
  178.8 3.4 %collective-permute-start.2 = (bf16[1,128,320]{1,2,0:T(8,128)(2,1)S(1)}, bf16[1,128,320]{1,2,0:T(8,128)(2,1)S(1)}, u32[]{:S(2)}, u32[]{:S(2)}) collective-permute-start(bf16[1,128,320]{1,2,0:T(8,128)(2,1)S(1)} %get-tuple-element.25), channel_id=1, source_target_pairs={{0,1},{2,3},{4,5},{6,7},{8,9},{10,11},{12,13},{14,15},{16,17},{18,... | collective-permute-start | bytes 245768 | tf_op jit(solution)/shard_map/ppermute | solution.py:14
  182.2 1.3 collective-permute-start.3
  183.5 97.6 %all-gather.5.cloned.1.call-done = bf16[4,9,25600]{1,0,2:T(4,128)(2,1)} async-done(((bf16[4,9,1600]{1,0,2:T(4,128)(2,1)}), bf16[4,9,25600]{1,0,2:T(4,128)(2,1)}) %all-gather.5.cloned.1.call-update) | async-done | bytes 1843216 | tf_op jit(solution)/shard_map/all_gather | solution.py:51
  281.1 29.7 %copy.78 = bf16[4,9,80,320]{3,2,0,1:T(8,128)(2,1)S(1)} copy(bf16[4,9,80,320]{1,0,3,2:T(4,128)(2,1)} %bitcast.135) | data formatting | bytes 3686400 | tf_op jit(solution)/shard_map/reshape | solution.py:46
  310.8 0.2 fusion.61
  311.1 0.0 collective-permute-done.2
  311.1 0.0 collective-permute-done.3
  311.2 0.3 select_maximum_fusion
  311.5 0.2 slice_bitcast_fusion.1
  312.0 0.4 fusion.22
  312.4 0.4 convolution_add_fusion.1
  312.9 0.0 copy-start.9
  312.9 0.4 convolution_add_fusion
  313.3 0.2 reshape.141
  313.5 0.1 copy-done.9
  313.5 0.8 fusion.50
  (27 shorter events, 0.5 us)
Async XLA Ops:
  6.5 3.3 %copy-start.3 = (bf16[4,9,1600]{2,0,1:T(4,128)(2,1)S(1)}, bf16[4,9,1600]{2,0,1:T(4,128)(2,1)}, u32[]{:S(2)}) copy-start(bf16[4,9,1600]{2,0,1:T(4,128)(2,1)} %param.26) | copy-start | bytes 345604
  6.5 139.5 %all-gather.3.cloned.1.call-start = ((), (), s32[]{:S(2)}) async-start(), calls=%async_computation | async-start | bytes 27852800 | tf_op jit(solution)/shard_map/all_gather | solution.py:51
  9.7 2.5 copy-start.11
  9.7 2.7 copy-start.12
  9.7 2.9 copy-start
  9.7 2.9 copy-start.4
  9.7 2.9 copy-start.5
  9.7 271.4 %all-gather.5.cloned.1.call-start = ((), (), s32[]{:S(2)}) async-start(), calls=%async_computation.1 | async-start | bytes 27852800 | tf_op jit(solution)/shard_map/all_gather | solution.py:51
  12.2 8.0 %copy-start.13 = (f32[1,32]{1,0:T(1,128)S(1)}, f32[1,32]{1,0:T(1,128)}, u32[]{:S(2)}) copy-start(f32[1,32]{1,0:T(1,128)} %param.23) | copy-start | bytes 388
  12.2 8.2 %copy-start.14 = (f32[1,32]{1,0:T(1,128)S(1)}, f32[1,32]{1,0:T(1,128)}, u32[]{:S(2)}) copy-start(f32[1,32]{1,0:T(1,128)} %param.22) | copy-start | bytes 388
  12.2 8.4 %copy-start.10 = (f32[1,320]{1,0:T(1,128)S(1)}, f32[1,320]{1,0:T(1,128)}, u32[]{:S(2)}) copy-start(f32[1,320]{1,0:T(1,128)} %param.21) | copy-start | bytes 3844
  12.9 7.7 %collective-permute-start = (bf16[1,128,320]{1,2,0:T(8,128)(2,1)S(1)}, bf16[1,128,320]{1,2,0:T(8,128)(2,1)S(1)}, u32[]{:S(2)}, u32[]{:S(2)}) collective-permute-start(bf16[1,128,320]{1,2,0:T(8,128)(2,1)S(1)} %get-tuple-element.29), channel_id=1, source_target_pairs={{0,1},{2,3},{4,5},{6,7},{8,9},{10,11},{12,13},{14,15},{16,17},{18,... | collective-permute-start | bytes 245768 | tf_op jit(solution)/shard_map/ppermute | solution.py:14
  17.8 6.3 %collective-permute-start.1 = (bf16[1,128,320]{1,2,0:T(8,128)(2,1)S(1)}, bf16[1,128,320]{1,2,0:T(8,128)(2,1)S(1)}, u32[]{:S(2)}, u32[]{:S(2)}) collective-permute-start(bf16[1,128,320]{1,2,0:T(8,128)(2,1)S(1)} %get-tuple-element.30), channel_id=1, source_target_pairs={{1,0},{3,2},{5,4},{7,6},{9,8},{11,10},{13,12},{15,14},{17,16},{19,... | collective-permute-start | bytes 245768 | tf_op jit(solution)/shard_map/ppermute | solution.py:15
  176.3 0.9 copy-start.1
  176.3 1.0 copy-start.2
  176.8 1.0 copy-start.6
  176.8 1.0 copy-start.7
  176.8 1.0 copy-start.8
  178.8 132.3 %collective-permute-start.2 = (bf16[1,128,320]{1,2,0:T(8,128)(2,1)S(1)}, bf16[1,128,320]{1,2,0:T(8,128)(2,1)S(1)}, u32[]{:S(2)}, u32[]{:S(2)}) collective-permute-start(bf16[1,128,320]{1,2,0:T(8,128)(2,1)S(1)} %get-tuple-element.25), channel_id=1, source_target_pairs={{0,1},{2,3},{4,5},{6,7},{8,9},{10,11},{12,13},{14,15},{16,17},{18,... | collective-permute-start | bytes 245768 | tf_op jit(solution)/shard_map/ppermute | solution.py:14
  182.2 128.9 %collective-permute-start.3 = (bf16[1,128,320]{1,2,0:T(8,128)(2,1)S(1)}, bf16[1,128,320]{1,2,0:T(8,128)(2,1)S(1)}, u32[]{:S(2)}, u32[]{:S(2)}) collective-permute-start(bf16[1,128,320]{1,2,0:T(8,128)(2,1)S(1)} %get-tuple-element.26), channel_id=1, source_target_pairs={{1,0},{3,2},{5,4},{7,6},{9,8},{11,10},{13,12},{15,14},{17,16},{19,... | collective-permute-start | bytes 245768 | tf_op jit(solution)/shard_map/ppermute | solution.py:15
  312.9 0.7 copy-start.9
Sparse Core Ops, SparseCore 0:
  9.8 136.1 all-gather.2
  147.6 133.4 all-gather.4
where the time goes:
time: 323 us; the launch traced here: 321 us
  waiting for transfers between devices  222 us (69%)
  local copies, waits for them, and re-layouts  68.9 us (21%)
  between operations  13.9 us (4%)
  starting transfers between devices  10.9 us (3%)
    all_gather x2, waiting for transfers between devices, whole_weights(): whole_kernel = lax.all_gather(kernel, 'dp', axis=2, tiled=True)  218 us
    reshape x2, local copies, waits for them, and re-layouts, reorder_whole(): split = whole_kernel.reshape(blocks, 9, channels // blocks, channels)  59.7 us
    ppermute x2, starting transfers between devices, padded_2(): before = lax.ppermute(last, axis, up)  8.29 us
    unnamed x34, local copies, waits for them, and re-layouts  6.57 us
  transfers between devices with their start and end apart: 6, of which 3 were waited for; matrix products, arithmetic and copies ran while one was open for 21% of the time, Pallas kernels for 0%

commit v1 on v0

--- a/solution.py
+++ b/solution.py
@@ -41,15 +41,35 @@
     return window.reshape(height * columns, depth)
 
 
-def reorder_whole(whole_kernel, channels):
-    blocks = whole_kernel.shape[0]
-    split = whole_kernel.reshape(blocks, 9, channels // blocks, channels)
-    return jnp.transpose(split, (1, 0, 2, 3)).reshape(3, 3 * channels, channels)
+def reorder_whole(gathered, channels):
+    devices, taps, blocks, length = gathered.shape
+    split = jnp.transpose(gathered, (1, 2, 0, 3))
+    return split.reshape(3, 3 * channels, channels)
+
+
+def gather_dense(shard, axis):
+    devices = lax.axis_size(axis)
+    if devices & (devices - 1):
+        return lax.all_gather(shard, axis, axis=0, tiled=False)
+    index = lax.axis_index(axis)
+    gathered = shard[None]
+    bit = devices // 2
+    while bit:
+        other = lax.ppermute(gathered, axis, [(i, i ^ bit) for i in range(devices)])
+        gathered = jnp.concatenate([gathered, other], axis=0)
+        bit //= 2
+    order = [0]
+    bit = devices // 2
+    while bit:
+        order = order + [i ^ bit for i in order]
+        bit //= 2
+    place = jnp.array([order.index(i) for i in range(devices)], jnp.int32)
+    return jnp.take(gathered, place[jnp.arange(devices) ^ index], axis=0)
 
 
 def whole_weights(kernel, channels):
-    whole_kernel = lax.all_gather(kernel, "dp", axis=2, tiled=True)
-    return reorder_whole(whole_kernel, channels)
+    dense = jnp.transpose(kernel, (1, 0, 2))
+    return reorder_whole(gather_dense(dense, "dp"), channels)
 
 
 def convolve_whole(activation, weights):

time: 323 us -> 97 us (0.30)
  waiting for transfers between devices: 222 us -> 21.5 us
  local copies, waits for them, and re-layouts: 68.9 us -> 40.6 us
  between operations: 13.9 us -> 0.64 us
  starting transfers between devices: 10.9 us -> 19.9 us
  other arithmetic: 2.98 us -> 9.64 us
    all_gather x2 -> x0, waiting for transfers between devices: 218 us -> none  [whole_weights(): whole_kernel = lax.all_gather(kernel, 'dp', axis=2, tiled=True)]
    reshape x2 -> x0, local copies, waits for them, and re-layouts: 59.7 us -> none  [reorder_whole(): split = whole_kernel.reshape(blocks, 9, channels // blocks, channels)]
    ppermute x0 -> x8, waiting for transfers between devices: none -> 20 us  [gather_dense(): other = lax.ppermute(gathered, axis, [(i, i ^ bit) for i in range(devices)])]
    gather x0 -> x3, local copies, waits for them, and re-layouts: none -> 10 us  [gather_dense(): return jnp.take(gathered, place[jnp.arange(devices) ^ index], axis=0)]
    ppermute x0 -> x8, starting transfers between devices: none -> 9.69 us  [gather_dense(): other = lax.ppermute(gathered, axis, [(i, i ^ bit) for i in range(devices)])]
    squeeze x0 -> x6, local copies, waits for them, and re-layouts: none -> 8.65 us  [convolve_whole(): weights[tap_row]]
    concatenate x0 -> x2, local copies, waits for them, and re-layouts: none -> 3.77 us  [gather_dense(): gathered = jnp.concatenate([gathered, other], axis=0)]
    slice x2 -> x7, local copies, waits for them, and re-layouts: 0.46 us -> 3.76 us  [convolve_whole(): weights[tap_row]]
  transfers between devices with their start and end apart: 6 -> 12, of which waited for: 3 -> 5; matrix products, arithmetic and copies ran while one was open for 21% -> 27% of each run, Pallas kernels for 0% -> 0%
where the time goes in v1:
time: 97 us; the launch traced here: 96.5 us
  local copies, waits for them, and re-layouts  40.6 us (42%)
  waiting for transfers between devices  21.5 us (22%)
  starting transfers between devices  19.9 us (21%)
  other arithmetic  9.64 us (10%)
  matrix products  4.16 us (4%)
    ppermute x8, waiting for transfers between devices, gather_dense(): other = lax.ppermute(gathered, axis, [(i, i ^ bit) for i in range(devices)])  20 us
    gather x3, local copies, waits for them, and re-layouts, gather_dense(): return jnp.take(gathered, place[jnp.arange(devices) ^ index], axis=0)  10 us
    ppermute x8, starting transfers between devices, gather_dense(): other = lax.ppermute(gathered, axis, [(i, i ^ bit) for i in range(devices)])  9.69 us
    squeeze x6, local copies, waits for them, and re-layouts, convolve_whole(): weights[tap_row]  8.65 us
    unnamed x52, local copies, waits for them, and re-layouts  7.98 us
    ppermute x2, starting transfers between devices, padded_2(): before = lax.ppermute(last, axis, up)  7.64 us
    dot_general x6, matrix products, convolve_whole(): jnp.dot(windows, weights[tap_row], preferred_element_type=jnp.float32)  4.16 us
    concatenate x2, local copies, waits for them, and re-layouts, gather_dense(): gathered = jnp.concatenate([gathered, other], axis=0)  3.77 us
  transfers between devices with their start and end apart: 12, of which 5 were waited for; matrix products, arithmetic and copies ran while one was open for 27% of the time, Pallas kernels for 0%

profile of v1, /device:TPU:0, one launch (start us, length us, event | category | flops | bytes accessed | tf_op | source)
XLA Modules:
  0.0 96.5 jit_solution(17578538265164025780)
XLA Ops:
  0.0 4.1 %collective-permute-start.8 = (bf16[1,9,4,1600]{3,2,1,0:T(4,128)(2,1)}, bf16[1,9,4,1600]{3,2,1,0:T(4,128)(2,1)S(1)}, u32[]{:S(2)}, u32[]{:S(2)}) collective-permute-start(bf16[1,9,4,1600]{3,2,1,0:T(4,128)(2,1)} %bitcast.151), channel_id=1, source_target_pairs={{0,16},{2,18},{4,20},{6,22},{8,24},{10,26},{12,28},{14,30},{16,0},... | collective-permute-start | bytes 345608 | tf_op jit(solution)/shard_map/ppermute | solution.py:58
  4.2 0.7 mul.80
  5.1 0.7 sub.41
  5.9 1.2 %multiply_convert_fusion.3 = bf16[2,128,320]{1,2,0:T(8,128)(2,1)S(1)} fusion(bf16[1,2,128,320]{2,3,1,0:T(8,128)(2,1)} %param.18, f32[320]{0:T(512)} %param.22, f32[320]{0:T(512)} %param.21, f32[320]{0:T(512)S(1)} %mul.81, f32[320]{0:T(512)S(1)} %sub.42), kind=kLoop, calls=%fused_computation.75 | loop fusion | flops 819200 | bytes 332800 | tf_op jit(solution)/shard_map/convert_element_type | solution.py:111
  7.1 3.7 %collective-permute-start = (bf16[1,128,320]{1,2,0:T(8,128)(2,1)S(1)}, bf16[1,128,320]{1,2,0:T(8,128)(2,1)S(1)}, u32[]{:S(2)}, u32[]{:S(2)}) collective-permute-start(bf16[1,128,320]{1,2,0:T(8,128)(2,1)S(1)} %get-tuple-element.30), channel_id=1, source_target_pairs={{0,1},{2,3},{4,5},{6,7},{8,9},{10,11},{12,13},{14,15},{16,17},{18,... | collective-permute-start | bytes 245768 | tf_op jit(solution)/shard_map/ppermute | solution.py:14
  10.8 1.3 %collective-permute-start.1 = (bf16[1,128,320]{1,2,0:T(8,128)(2,1)S(1)}, bf16[1,128,320]{1,2,0:T(8,128)(2,1)S(1)}, u32[]{:S(2)}, u32[]{:S(2)}) collective-permute-start(bf16[1,128,320]{1,2,0:T(8,128)(2,1)S(1)} %get-tuple-element.31), channel_id=1, source_target_pairs={{1,0},{3,2},{5,4},{7,6},{9,8},{11,10},{13,12},{15,14},{17,16},{19,... | collective-permute-start | bytes 245768 | tf_op jit(solution)/shard_map/ppermute | solution.py:15
  12.1 1.6 %constant_dynamic-update-slice_fusion.9 = bf16[16,9,4,1600]{3,2,1,0:T(4,128)(2,1)} fusion(bf16[4,9,1600]{2,0,1:T(4,128)(2,1)} %param.30), kind=kLoop, calls=%fused_computation.123 | loop fusion | bytes 235008
  13.7 0.9 constant_dynamic-update-slice_fusion.4
  14.7 1.3 %gather_fusion = s32[16]{0:T(128)S(1)} fusion(s32[16]{0:T(128)} %constant.29.clone, s32[1024]{0:T(1024)S(1)} %pad_clamp_fusion.1), kind=kCustom, calls=%fused_computation.2 | custom fusion | bytes 192 | tf_op jit(solution)/shard_map/gather | solution.py:67
  16.0 1.1 %copy.29 = f32[1,2,128,320]{2,1,3,0:T(2,128)S(1)} copy(bf16[1,2,128,320]{2,3,1,0:T(8,128)(2,1)} %param.18) | data formatting | bytes 491520 | tf_op jit(solution)/shard_map/convert_element_type | solution.py:110
  17.1 0.9 multiply_convert_fusion.2
  18.5 0.3 fusion.5
  18.8 0.2 slice_bitcast_fusion.7
  19.0 0.7 copy_bitcast_fusion.13
  19.8 0.7 copy_bitcast_fusion.9
  20.5 0.8 copy_bitcast_fusion.11
  21.2 0.8 copy_bitcast_fusion.8
  22.0 0.2 pad_maximum_fusion.5
  22.2 1.6 %collective-permute-start.9 = (bf16[2,9,4,1600]{3,2,1,0:T(4,128)(2,1)S(1)}, bf16[2,9,4,1600]{3,2,1,0:T(4,128)(2,1)S(1)}, u32[]{:S(2)}, u32[]{:S(2)}) collective-permute-start(bf16[2,9,4,1600]{3,2,1,0:T(4,128)(2,1)S(1)} %pad_maximum_fusion.5), channel_id=1, source_target_pairs={{0,8},{2,10},{4,12},{6,14},{8,0},{10,2},{12,4},{14,6},{16,24},{18,... | collective-permute-start | bytes 691208 | tf_op jit(solution)/shard_map/ppermute | solution.py:58
  23.8 0.2 pad_maximum_fusion.4
  24.0 0.5 collective-permute-start.3
  24.5 0.7 constant_dynamic-update-slice_fusion.8
  25.2 5.7 %collective-permute-done.9 = bf16[2,9,4,1600]{3,2,1,0:T(4,128)(2,1)S(1)} collective-permute-done((bf16[2,9,4,1600]{3,2,1,0:T(4,128)(2,1)S(1)}, bf16[2,9,4,1600]{3,2,1,0:T(4,128)(2,1)S(1)}, u32[]{:S(2)}, u32[]{:S(2)}) %collective-permute-start.9) | collective-permute-done | bytes 230432 | tf_op jit(solution)/shard_map/ppermute | solution.py:58
  30.9 0.3 pad_maximum_fusion.3
  31.3 1.6 %collective-permute-start.10 = (bf16[4,9,4,1600]{3,2,1,0:T(4,128)(2,1)S(1)}, bf16[4,9,4,1600]{3,2,1,0:T(4,128)(2,1)S(1)}, u32[]{:S(2)}, u32[]{:S(2)}) collective-permute-start(bf16[4,9,4,1600]{3,2,1,0:T(4,128)(2,1)S(1)} %pad_maximum_fusion.3), channel_id=1, source_target_pairs={{0,4},{2,6},{4,0},{6,2},{8,12},{10,14},{12,8},{14,10},{16,20},{18,... | collective-permute-start | bytes 1382408 | tf_op jit(solution)/shard_map/ppermute | solution.py:58
  32.9 1.2 %collective-permute-done.3 = bf16[2,9,4,1600]{3,2,1,0:T(4,128)(2,1)S(1)} collective-permute-done((bf16[2,9,4,1600]{3,2,1,0:T(4,128)(2,1)S(1)}, bf16[2,9,4,1600]{3,2,1,0:T(4,128)(2,1)S(1)}, u32[]{:S(2)}, u32[]{:S(2)}) %collective-permute-start.3) | collective-permute-done | bytes 230432 | tf_op jit(solution)/shard_map/ppermute | solution.py:58
  34.1 0.3 pad_maximum_fusion.2
  34.5 1.6 %collective-permute-start.4 = (bf16[4,9,4,1600]{3,2,1,0:T(4,128)(2,1)S(1)}, bf16[4,9,4,1600]{3,2,1,0:T(4,128)(2,1)S(1)}, u32[]{:S(2)}, u32[]{:S(2)}) collective-permute-start(bf16[4,9,4,1600]{3,2,1,0:T(4,128)(2,1)S(1)} %pad_maximum_fusion.2), channel_id=1, source_target_pairs={{0,4},{2,6},{4,0},{6,2},{8,12},{10,14},{12,8},{14,10},{16,20},{18,... | collective-permute-start | bytes 1382408 | tf_op jit(solution)/shard_map/ppermute | solution.py:58
  36.0 0.8 constant_dynamic-update-slice_fusion.7
  36.8 8.3 %collective-permute-done.10 = bf16[4,9,4,1600]{3,2,1,0:T(4,128)(2,1)S(1)} collective-permute-done((bf16[4,9,4,1600]{3,2,1,0:T(4,128)(2,1)S(1)}, bf16[4,9,4,1600]{3,2,1,0:T(4,128)(2,1)S(1)}, u32[]{:S(2)}, u32[]{:S(2)}) %collective-permute-start.10) | collective-permute-done | bytes 460832 | tf_op jit(solution)/shard_map/ppermute | solution.py:58
  45.2 0.7 pad_maximum_fusion.1
  45.9 4.7 %collective-permute-done.4 = bf16[4,9,4,1600]{3,2,1,0:T(4,128)(2,1)S(1)} collective-permute-done((bf16[4,9,4,1600]{3,2,1,0:T(4,128)(2,1)S(1)}, bf16[4,9,4,1600]{3,2,1,0:T(4,128)(2,1)S(1)}, u32[]{:S(2)}, u32[]{:S(2)}) %collective-permute-start.4) | collective-permute-done | bytes 460832 | tf_op jit(solution)/shard_map/ppermute | solution.py:58
  50.7 0.7 pad_maximum_fusion
  51.6 0.9 constant_dynamic-update-slice_fusion.6
  52.5 0.2 constant_dynamic-update-slice_fusion.1
  52.7 1.3 %copy-done = bf16[16,9,4,1600]{3,2,1,0:T(4,128)(2,1)} copy-done((bf16[16,9,4,1600]{3,2,1,0:T(4,128)(2,1)}, bf16[16,9,4,1600]{3,2,1,0:T(4,128)(2,1)S(1)}, u32[]{:S(2)}) %copy-start) | copy-done | bytes 1843224
  54.0 1.3 %constant_dynamic-update-slice_fusion.5 = bf16[16,9,4,1600]{3,2,1,0:T(4,128)(2,1)} fusion(bf16[16,9,4,1600]{3,2,1,0:T(4,128)(2,1)} %constant_dynamic-update-slice_fusion.6, bf16[8,9,4,1600]{3,2,1,0:T(4,128)(2,1)S(1)} %collective-permute-done.11), kind=kLoop, calls=%fused_computation.119 | loop fusion | bytes 1880064 | tf_op jit(solution)/shard_map/concatenate | solution.py:59
  55.3 3.8 %gather_fusion.2 = bf16[16,9,4,1600]{3,2,1,0:T(4,128)(2,1)S(1)} fusion(bf16[16,9,4,1600]{3,2,1,0:T(4,128)(2,1)} %constant_dynamic-update-slice_fusion.5, s32[1024]{0:T(1024)S(1)} %pad_clamp_fusion), kind=kCustom, calls=%fused_computation.1.clone | custom fusion | bytes 3686464 | tf_op jit(solution)/shard_map/jit(_take)/gather | solution.py:67
  59.1 2.5 %constant_dynamic-update-slice_fusion = bf16[16,9,4,1600]{3,2,1,0:T(4,128)(2,1)} fusion(bf16[16,9,4,1600]{3,2,1,0:T(4,128)(2,1)} %copy-done, bf16[8,9,4,1600]{3,2,1,0:T(4,128)(2,1)} %collective-permute-done.5), kind=kLoop, calls=%fused_computation.114 | loop fusion | bytes 1916928 | tf_op jit(solution)/shard_map/concatenate | solution.py:59
  61.6 4.9 %gather_fusion.1 = bf16[16,9,4,1600]{3,2,1,0:T(4,128)(2,1)} fusion(bf16[16,9,4,1600]{3,2,1,0:T(4,128)(2,1)} %constant_dynamic-update-slice_fusion, s32[1024]{0:T(1024)S(1)} %pad_clamp_fusion), kind=kCustom, calls=%fused_computation.clone | custom fusion | bytes 3686464 | tf_op jit(solution)/shard_map/jit(_take)/gather | solution.py:67
  66.5 3.3 %select_bitcast_fusion.1 = (bf16[9,4,16,1600]{3,1,0,2:T(4,128)(2,1)S(1)}, bf16[9,4,16,1600]{3,1,0,2:T(4,128)(2,1)S(1)}) fusion(bf16[16,9,4,1600]{3,2,1,0:T(4,128)(2,1)} %gather_fusion.1, pred[16]{0:T(512)(128)(4,1)S(1)} %compare_and_fusion, bf16[16,9,4,1600]{3,2,1,0:T(4,128)(2,1)S(1)} %gather_fusion.2), kind=kLoop, calls=%fused_computation.6 | loop fusion | flops 1843200 | bytes 7372816 | tf_op jit(solution)/shard_map/transpose | solution.py:46
  69.7 2.3 %fusion.62 = (bf16[3,4,16,1600]{3,1,0,2:T(4,128)(2,1)S(1)}, bf16[3,4,16,1600]{3,1,0,2:T(4,128)(2,1)S(1)}, bf16[3,4,16,1600]{3,1,0,2:T(4,128)(2,1)S(1)}, bf16[3,4...) fusion(bf16[9,4,16,1600]{3,1,0,2:T(4,128)(2,1)S(1)} %get-tuple-element.33, ...), kind=kLoop, calls=%fused_computation.136 | loop fusion | bytes 7372800 | tf_op jit(solution)/shard_map/slice | solution.py:88
  72.1 1.7 %squeeze.19 = bf16[960,320]{1,0:T(8,128)(2,1)} reshape(bf16[3,4,16,1600]{3,2,1,0:T(8,128)(2,1)S(1)} %copy.27) | data formatting | bytes 1228800 | tf_op jit(solution)/shard_map/squeeze | solution.py:88
  73.8 1.1 %copy.31 = bf16[3,4,16,1600]{3,2,1,0:T(8,128)(2,1)S(1)} copy(bf16[3,4,16,1600]{3,1,0,2:T(4,128)(2,1)} %get-tuple-element.37) | data formatting | bytes 1228800 | tf_op jit(solution)/shard_map/slice | solution.py:88
  75.0 1.7 %squeeze.20 = bf16[960,320]{1,0:T(8,128)(2,1)} reshape(bf16[3,4,16,1600]{3,2,1,0:T(8,128)(2,1)S(1)} %copy.31) | data formatting | bytes 1228800 | tf_op jit(solution)/shard_map/squeeze | solution.py:88
  76.8 1.7 %squeeze.21 = bf16[960,320]{1,0:T(8,128)(2,1)} reshape(bf16[3,4,16,1600]{3,2,1,0:T(8,128)(2,1)S(1)} %copy.35) | data formatting | bytes 1228800 | tf_op jit(solution)/shard_map/squeeze | solution.py:88
  78.6 1.8 %fusion.6 = f32[256,320]{0,1:T(8,128)S(1)} fusion(bf16[960,320]{1,0:T(8,128)(2,1)} %squeeze.19, bf16[256,320]{0,1:T(8,128)(2,1)S(1)} %get-tuple-element.43, bf16[256,320]{0,1:T(8,128)(2,1)} %get-tuple-element.46, bf16[256,320]{0,1:T(8,128)(2,1)} %get-tuple-element.44), kind=kOutput, calls=%fused_computation.21 | convolution fusion | flops 158760960 | bytes 1433600 | tf_op jit(solution)/shard_map/dot_general | solution.py:87
  80.5 0.4 convolution_add_fusion.3
  81.0 0.6 multiply_convert_fusion
  81.6 0.3 multiply_convert_fusion.1
  82.0 4.0 %collective-permute-start.6 = (bf16[1,128,320]{1,2,0:T(8,128)(2,1)S(1)}, bf16[1,128,320]{1,2,0:T(8,128)(2,1)S(1)}, u32[]{:S(2)}, u32[]{:S(2)}) collective-permute-start(bf16[1,128,320]{1,2,0:T(8,128)(2,1)S(1)} %get-tuple-element.26), channel_id=1, source_target_pairs={{0,1},{2,3},{4,5},{6,7},{8,9},{10,11},{12,13},{14,15},{16,17},{18,... | collective-permute-start | bytes 245768 | tf_op jit(solution)/shard_map/ppermute | solution.py:14
  85.9 1.3 %collective-permute-start.7 = (bf16[1,128,320]{1,2,0:T(8,128)(2,1)S(1)}, bf16[1,128,320]{1,2,0:T(8,128)(2,1)S(1)}, u32[]{:S(2)}, u32[]{:S(2)}) collective-permute-start(bf16[1,128,320]{1,2,0:T(8,128)(2,1)S(1)} %get-tuple-element.27), channel_id=1, source_target_pairs={{1,0},{3,2},{5,4},{7,6},{9,8},{11,10},{13,12},{15,14},{17,16},{19,... | collective-permute-start | bytes 245768 | tf_op jit(solution)/shard_map/ppermute | solution.py:15
  87.3 1.7 %squeeze.22 = bf16[960,320]{1,0:T(8,128)(2,1)} reshape(bf16[3,4,16,1600]{3,2,1,0:T(8,128)(2,1)S(1)} %copy.40) | data formatting | bytes 1228800 | tf_op jit(solution)/shard_map/squeeze | solution.py:88
  89.1 0.9 squeeze.23
  90.1 0.9 squeeze.24
  90.9 1.5 %collective-permute-done.7 = bf16[1,128,320]{1,2,0:T(8,128)(2,1)S(1)} collective-permute-done((bf16[1,128,320]{1,2,0:T(8,128)(2,1)S(1)}, bf16[1,128,320]{1,2,0:T(8,128)(2,1)S(1)}, u32[]{:S(2)}, u32[]{:S(2)}) %collective-permute-start.7) | collective-permute-done | bytes 81952 | tf_op jit(solution)/shard_map/ppermute | solution.py:15
  92.5 0.3 select_maximum_fusion
  92.8 0.2 slice_bitcast_fusion.1
  93.3 0.6 copy-done.4
  93.9 0.4 fusion.22
  94.3 0.4 convolution_add_fusion.1
  94.8 0.4 convolution_add_fusion
  95.4 0.3 copy-done.3
  95.7 0.8 fusion.50
  (81 shorter events, 1.9 us)
Async XLA Ops:
  0.0 17.1 %copy-start.13 = (f32[320]{0:T(512)S(1)}, f32[320]{0:T(512)}, u32[]{:S(2)}) copy-start(f32[320]{0:T(512)} %param.21) | copy-start | bytes 3844
  0.0 17.1 %copy-start.12 = (f32[320]{0:T(512)S(1)}, f32[320]{0:T(512)}, u32[]{:S(2)}) copy-start(f32[320]{0:T(512)} %param.22) | copy-start | bytes 3844
  0.0 18.0 %copy-start.19 = (f32[1,32]{1,0:T(1,128)S(1)}, f32[1,32]{1,0:T(1,128)}, u32[]{:S(2)}) copy-start(f32[1,32]{1,0:T(1,128)} %param.27) | copy-start | bytes 388
  0.0 18.2 %copy-start.20 = (f32[1,32]{1,0:T(1,128)S(1)}, f32[1,32]{1,0:T(1,128)}, u32[]{:S(2)}) copy-start(f32[1,32]{1,0:T(1,128)} %param.26) | copy-start | bytes 388
  0.0 18.4 %copy-start.18 = (f32[1,320]{1,0:T(1,128)S(1)}, f32[1,320]{1,0:T(1,128)}, u32[]{:S(2)}) copy-start(f32[1,320]{1,0:T(1,128)} %param.25) | copy-start | bytes 3844
  0.0 22.0 %collective-permute-start.8 = (bf16[1,9,4,1600]{3,2,1,0:T(4,128)(2,1)}, bf16[1,9,4,1600]{3,2,1,0:T(4,128)(2,1)S(1)}, u32[]{:S(2)}, u32[]{:S(2)}) collective-permute-start(bf16[1,9,4,1600]{3,2,1,0:T(4,128)(2,1)} %bitcast.151), channel_id=1, source_target_pairs={{0,16},{2,18},{4,20},{6,22},{8,24},{10,26},{12,28},{14,30},{16,0},... | collective-permute-start | bytes 345608 | tf_op jit(solution)/shard_map/ppermute | solution.py:58
  4.2 19.6 %collective-permute-start.2 = (bf16[1,9,4,1600]{3,2,1,0:T(4,128)(2,1)}, bf16[1,9,4,1600]{3,2,1,0:T(4,128)(2,1)S(1)}, u32[]{:S(2)}, u32[]{:S(2)}) collective-permute-start(bf16[1,9,4,1600]{3,2,1,0:T(4,128)(2,1)} %bitcast.155), channel_id=1, source_target_pairs={{0,16},{2,18},{4,20},{6,22},{8,24},{10,26},{12,28},{14,30},{16,0},... | collective-permute-start | bytes 345608 | tf_op jit(solution)/shard_map/ppermute | solution.py:58
  7.1 11.3 %collective-permute-start = (bf16[1,128,320]{1,2,0:T(8,128)(2,1)S(1)}, bf16[1,128,320]{1,2,0:T(8,128)(2,1)S(1)}, u32[]{:S(2)}, u32[]{:S(2)}) collective-permute-start(bf16[1,128,320]{1,2,0:T(8,128)(2,1)S(1)} %get-tuple-element.30), channel_id=1, source_target_pairs={{0,1},{2,3},{4,5},{6,7},{8,9},{10,11},{12,13},{14,15},{16,17},{18,... | collective-permute-start | bytes 245768 | tf_op jit(solution)/shard_map/ppermute | solution.py:14
  10.8 7.7 %collective-permute-start.1 = (bf16[1,128,320]{1,2,0:T(8,128)(2,1)S(1)}, bf16[1,128,320]{1,2,0:T(8,128)(2,1)S(1)}, u32[]{:S(2)}, u32[]{:S(2)}) collective-permute-start(bf16[1,128,320]{1,2,0:T(8,128)(2,1)S(1)} %get-tuple-element.31), channel_id=1, source_target_pairs={{1,0},{3,2},{5,4},{7,6},{9,8},{11,10},{13,12},{15,14},{17,16},{19,... | collective-permute-start | bytes 245768 | tf_op jit(solution)/shard_map/ppermute | solution.py:15
  19.0 3.0 %copy-start.1 = (bf16[4,9,1600]{2,0,1:T(4,128)(2,1)S(1)}, bf16[4,9,1600]{2,0,1:T(4,128)(2,1)}, u32[]{:S(2)}) copy-start(bf16[4,9,1600]{2,0,1:T(4,128)(2,1)} %param.30) | copy-start | bytes 345604
  19.0 4.8 %copy-start.2 = (bf16[4,9,1600]{2,0,1:T(4,128)(2,1)S(1)}, bf16[4,9,1600]{2,0,1:T(4,128)(2,1)}, u32[]{:S(2)}) copy-start(bf16[4,9,1600]{2,0,1:T(4,128)(2,1)} %param.23) | copy-start | bytes 345604
  22.2 8.8 %collective-permute-start.9 = (bf16[2,9,4,1600]{3,2,1,0:T(4,128)(2,1)S(1)}, bf16[2,9,4,1600]{3,2,1,0:T(4,128)(2,1)S(1)}, u32[]{:S(2)}, u32[]{:S(2)}) collective-permute-start(bf16[2,9,4,1600]{3,2,1,0:T(4,128)(2,1)S(1)} %pad_maximum_fusion.5), channel_id=1, source_target_pairs={{0,8},{2,10},{4,12},{6,14},{8,0},{10,2},{12,4},{14,6},{16,24},{18,... | collective-permute-start | bytes 691208 | tf_op jit(solution)/shard_map/ppermute | solution.py:58
  24.0 10.1 %collective-permute-start.3 = (bf16[2,9,4,1600]{3,2,1,0:T(4,128)(2,1)S(1)}, bf16[2,9,4,1600]{3,2,1,0:T(4,128)(2,1)S(1)}, u32[]{:S(2)}, u32[]{:S(2)}) collective-permute-start(bf16[2,9,4,1600]{3,2,1,0:T(4,128)(2,1)S(1)} %pad_maximum_fusion.4), channel_id=1, source_target_pairs={{0,8},{2,10},{4,12},{6,14},{8,0},{10,2},{12,4},{14,6},{16,24},{18,... | collective-permute-start | bytes 691208 | tf_op jit(solution)/shard_map/ppermute | solution.py:58
  31.3 13.9 %collective-permute-start.10 = (bf16[4,9,4,1600]{3,2,1,0:T(4,128)(2,1)S(1)}, bf16[4,9,4,1600]{3,2,1,0:T(4,128)(2,1)S(1)}, u32[]{:S(2)}, u32[]{:S(2)}) collective-permute-start(bf16[4,9,4,1600]{3,2,1,0:T(4,128)(2,1)S(1)} %pad_maximum_fusion.3), channel_id=1, source_target_pairs={{0,4},{2,6},{4,0},{6,2},{8,12},{10,14},{12,8},{14,10},{16,20},{18,... | collective-permute-start | bytes 1382408 | tf_op jit(solution)/shard_map/ppermute | solution.py:58
  34.5 16.2 %collective-permute-start.4 = (bf16[4,9,4,1600]{3,2,1,0:T(4,128)(2,1)S(1)}, bf16[4,9,4,1600]{3,2,1,0:T(4,128)(2,1)S(1)}, u32[]{:S(2)}, u32[]{:S(2)}) collective-permute-start(bf16[4,9,4,1600]{3,2,1,0:T(4,128)(2,1)S(1)} %pad_maximum_fusion.2), channel_id=1, source_target_pairs={{0,4},{2,6},{4,0},{6,2},{8,12},{10,14},{12,8},{14,10},{16,20},{18,... | collective-permute-start | bytes 1382408 | tf_op jit(solution)/shard_map/ppermute | solution.py:58
  45.9 6.9 %collective-permute-start.11 = (bf16[8,9,4,1600]{3,2,1,0:T(4,128)(2,1)S(1)}, bf16[8,9,4,1600]{3,2,1,0:T(4,128)(2,1)S(1)}, u32[]{:S(2)}, u32[]{:S(2)}) collective-permute-start(bf16[8,9,4,1600]{3,2,1,0:T(4,128)(2,1)S(1)} %pad_maximum_fusion.1), channel_id=1, source_target_pairs={{0,2},{2,0},{4,6},{6,4},{8,10},{10,8},{12,14},{14,12},{16,18},{18,... | collective-permute-start | bytes 2764808 | tf_op jit(solution)/shard_map/ppermute | solution.py:58
  51.4 7.7 %collective-permute-start.5 = (bf16[8,9,4,1600]{3,2,1,0:T(4,128)(2,1)S(1)}, bf16[8,9,4,1600]{3,2,1,0:T(4,128)(2,1)}, u32[]{:S(2)}, u32[]{:S(2)}) collective-permute-start(bf16[8,9,4,1600]{3,2,1,0:T(4,128)(2,1)S(1)} %pad_maximum_fusion), channel_id=1, source_target_pairs={{0,2},{2,0},{4,6},{6,4},{8,10},{10,8},{12,14},{14,12},{16,18},{18,... | collective-permute-start | bytes 2764808 | tf_op jit(solution)/shard_map/ppermute | solution.py:58
  52.7 1.3 %copy-start = (bf16[16,9,4,1600]{3,2,1,0:T(4,128)(2,1)}, bf16[16,9,4,1600]{3,2,1,0:T(4,128)(2,1)S(1)}, u32[]{:S(2)}) copy-start(bf16[16,9,4,1600]{3,2,1,0:T(4,128)(2,1)S(1)} %constant_dynamic-update-slice_fusion.1) | copy-start | bytes 5529604
  76.8 3.7 %copy-start.9 = (bf16[256,320]{0,1:T(8,128)(2,1)S(1)}, bf16[256,320]{0,1:T(8,128)(2,1)}, u32[]{:S(2)}) copy-start(bf16[256,320]{0,1:T(8,128)(2,1)} %get-tuple-element.41) | copy-start | bytes 491524
  78.5 1.9 %copy-start.6 = (bf16[960,320]{1,0:T(8,128)(2,1)S(1)}, bf16[960,320]{1,0:T(8,128)(2,1)}, u32[]{:S(2)}) copy-start(bf16[960,320]{1,0:T(8,128)(2,1)} %squeeze.20) | copy-start | bytes 1843204
  78.5 1.9 %copy-start.10 = (bf16[256,320]{0,1:T(8,128)(2,1)S(1)}, bf16[256,320]{0,1:T(8,128)(2,1)}, u32[]{:S(2)}) copy-start(bf16[256,320]{0,1:T(8,128)(2,1)} %get-tuple-element.42) | copy-start | bytes 491524
  78.5 1.9 %copy-start.11 = (bf16[256,320]{0,1:T(8,128)(2,1)S(1)}, bf16[256,320]{0,1:T(8,128)(2,1)}, u32[]{:S(2)}) copy-start(bf16[256,320]{0,1:T(8,128)(2,1)} %multiply_convert_fusion.2) | copy-start | bytes 491524
  78.5 2.4 %copy-start.5 = (bf16[960,320]{1,0:T(8,128)(2,1)S(1)}, bf16[960,320]{1,0:T(8,128)(2,1)}, u32[]{:S(2)}) copy-start(bf16[960,320]{1,0:T(8,128)(2,1)} %squeeze.21) | copy-start | bytes 1843204
  78.5 2.4 %copy-start.7 = (bf16[256,320]{0,1:T(8,128)(2,1)S(1)}, bf16[256,320]{0,1:T(8,128)(2,1)}, u32[]{:S(2)}) copy-start(bf16[256,320]{0,1:T(8,128)(2,1)} %get-tuple-element.39) | copy-start | bytes 491524
  78.5 2.4 %copy-start.8 = (bf16[256,320]{0,1:T(8,128)(2,1)S(1)}, bf16[256,320]{0,1:T(8,128)(2,1)}, u32[]{:S(2)}) copy-start(bf16[256,320]{0,1:T(8,128)(2,1)} %get-tuple-element.40) | copy-start | bytes 491524
  78.6 2.4 %copy-start.14 = (f32[320]{0:T(512)S(1)}, f32[320]{0:T(512)}, u32[]{:S(2)}) copy-start(f32[320]{0:T(512)} %param.29) | copy-start | bytes 3844
  78.6 2.4 %copy-start.15 = (f32[320]{0:T(512)S(1)}, f32[320]{0:T(512)}, u32[]{:S(2)}) copy-start(f32[320]{0:T(512)} %param.28) | copy-start | bytes 3844
  78.6 2.4 %copy-start.16 = (f32[320]{0:T(512)S(1)}, f32[320]{0:T(512)}, u32[]{:S(2)}) copy-start(f32[320]{0:T(512)} %param.24) | copy-start | bytes 3844
  82.0 9.0 %collective-permute-start.6 = (bf16[1,128,320]{1,2,0:T(8,128)(2,1)S(1)}, bf16[1,128,320]{1,2,0:T(8,128)(2,1)S(1)}, u32[]{:S(2)}, u32[]{:S(2)}) collective-permute-start(bf16[1,128,320]{1,2,0:T(8,128)(2,1)S(1)} %get-tuple-element.26), channel_id=1, source_target_pairs={{0,1},{2,3},{4,5},{6,7},{8,9},{10,11},{12,13},{14,15},{16,17},{18,... | collective-permute-start | bytes 245768 | tf_op jit(solution)/shard_map/ppermute | solution.py:14
  85.9 6.5 %collective-permute-start.7 = (bf16[1,128,320]{1,2,0:T(8,128)(2,1)S(1)}, bf16[1,128,320]{1,2,0:T(8,128)(2,1)S(1)}, u32[]{:S(2)}, u32[]{:S(2)}) collective-permute-start(bf16[1,128,320]{1,2,0:T(8,128)(2,1)S(1)} %get-tuple-element.27), channel_id=1, source_target_pairs={{1,0},{3,2},{5,4},{7,6},{9,8},{11,10},{13,12},{15,14},{17,16},{19,... | collective-permute-start | bytes 245768 | tf_op jit(solution)/shard_map/ppermute | solution.py:15
  92.8 1.1 %copy-start.4 = (bf16[960,320]{1,0:T(8,128)(2,1)S(1)}, bf16[960,320]{1,0:T(8,128)(2,1)}, u32[]{:S(2)}) copy-start(bf16[960,320]{1,0:T(8,128)(2,1)} %squeeze.22) | copy-start | bytes 1843204
  94.8 0.9 copy-start.3
  94.8 0.9 copy-start.17

commit v2 on v1

--- a/solution.py
+++ b/solution.py
@@ -1,7 +1,16 @@
+import functools
+
 import jax
 import jax.numpy as jnp
 from jax import lax
+from jax.experimental import pallas as pl
+from jax.experimental.pallas import tpu as pltpu
 from jax.sharding import PartitionSpec as P
+
+F32 = jnp.float32
+BF16 = jnp.bfloat16
+TAPS = 9
+SLAB = 16
 
 
 def padded_2(array, sides, width):
@@ -117,6 +126,320 @@
     return result.astype(jnp.bfloat16)[None]
 
 
+def call(body, out_shapes, moved, flops=0, scratch=()):
+    return pl.pallas_call(
+        body,
+        out_shape=out_shapes,
+        scratch_shapes=list(scratch),
+        cost_estimate=pl.CostEstimate(flops=flops, bytes_accessed=moved, transcendentals=0),
+        compiler_params=pltpu.CompilerParams(vmem_limit_bytes=48 << 20),
+    )
+
+
+def prepare_body(width, first_ref, second_ref, first_out, second_out):
+    half = lax.axis_index("rows")
+    blocks = second_out.shape[1]
+    for which in range(2):
+
+        @pl.when(half == which)
+        def _():
+            for step in range(first_out.shape[2] // width):
+                source = (2 * step + which) * width
+                first_out[:, :, step * width : (step + 1) * width] = first_ref[
+                    :, :, source : source + width
+                ]
+            second_out[...] = second_ref[:, which * blocks : (which + 1) * blocks, :]
+
+
+def merge_body(*refs):
+    out_ref = refs[-1]
+    depth = refs[0].shape[1]
+    for place, ref in enumerate(refs[:-1]):
+        out_ref[:, place * depth : (place + 1) * depth, :] = ref[...]
+
+
+def selection(steps, span, far, copies, channels):
+    blocks = channels // span
+    group = 4 * far * blocks
+    tail = copies * group
+    columns = (steps - 1) * group + tail
+    row = lax.broadcasted_iota(jnp.int32, (channels, columns), 0)
+    column = lax.broadcasted_iota(jnp.int32, (1, columns), 1)
+    step = jnp.minimum(column // group, steps - 1)
+    within = column % group
+    near = within // (far * blocks)
+    place = (within // blocks) % far
+    block = within % blocks
+    other = place * 4 + (near % 2) * 2 + near // 2
+    device = jnp.bitwise_xor(lax.axis_index("dp"), other)
+    source = block * span + device * steps + step
+    return jnp.where(row == source, 1.0, 0.0).astype(BF16)
+
+
+def silu(values):
+    return values / (1.0 + jnp.exp(-values))
+
+
+def store_slabs(out_ref, row, values):
+    slabs = values.shape[0]
+    out_ref[row, 1 : slabs + 1] = values.astype(BF16)
+    zero = jnp.zeros((1, values.shape[2]), F32)
+    before = jnp.concatenate([zero, values[slabs - 1, :-1]], axis=0)
+    after = jnp.concatenate([values[0, 1:], zero], axis=0)
+    out_ref[row, 0] = before.astype(BF16)
+    out_ref[row, slabs + 1] = after.astype(BF16)
+
+
+def first_body(steps, span, mine_ref, other_ref, norm_ref, out_ref, turned_ref):
+    half = lax.axis_index("rows")
+    local, channels, columns = mine_ref.shape
+    slabs = columns // SLAB
+    height = 2 * local
+    select = selection(steps, span, 4, 2, channels)
+    width = select.shape[1]
+    padding = jnp.zeros((-channels % 128, columns), F32)
+    edge = jnp.zeros(out_ref.shape[1:], BF16)
+    out_ref[0] = edge
+    out_ref[height + 1] = edge
+    mean, rstd = norm_ref[0:1, :], norm_ref[1:2, :]
+    gain, shift = norm_ref[2:3, :], norm_ref[3:4, :]
+    for source, base in ((mine_ref, half * local), (other_ref, (1 - half) * local)):
+        for row in range(local):
+            wide = jnp.concatenate([source[row].astype(F32), padding], axis=0)
+            sample = wide.T[:, :channels]
+            value = ((sample - mean) * rstd) * gain + shift
+            value = jnp.concatenate([silu(value), wide.T[:, channels:]], axis=1)
+            for tile in range(turned_ref.shape[0]):
+                turned_ref[tile] = value[:, tile * 128 : (tile + 1) * 128]
+            active = jnp.concatenate(
+                [
+                    jnp.concatenate(
+                        [
+                            turned_ref[tile, pl.ds(slab, SLAB, stride=slabs), :]
+                            for slab in range(slabs)
+                        ],
+                        axis=0,
+                    )
+                    for tile in range(turned_ref.shape[0])
+                ],
+                axis=1,
+            )[:, :channels].astype(BF16)
+            ordered = jnp.dot(active, select, preferred_element_type=F32)
+            store_slabs(out_ref, base + row + 1, ordered.reshape(slabs, SLAB, width))
+
+
+def window(ref, first, rows, slabs, tap, low, high):
+    tap_row, tap_col = tap // 3, tap % 3
+    block = ref[pl.ds(first + tap_row, rows), tap_col : tap_col + slabs, :, low:high]
+    return block.reshape(rows * slabs * SLAB, high - low)
+
+
+def tails(ref, first, rows, slabs, low, group):
+    copies = 128 // group
+    lane = lax.broadcasted_iota(jnp.int32, (1, 128), 1) // group
+    pieces = []
+    for start in range(0, TAPS, copies):
+        taps = range(start, min(start + copies, TAPS))
+        piece = window(ref, first, rows, slabs, start, low, low + 128)
+        for position, tap in enumerate(taps):
+            if position:
+                piece = jnp.where(
+                    lane >= position, window(ref, first, rows, slabs, tap, low, low + 128), piece
+                )
+        pieces.append(piece[:, : len(taps) * group])
+    return jnp.concatenate(pieces, axis=1)
+
+
+def place_weights(gathered, main_ref, tail_ref, steps, width):
+    depth = gathered[0].shape[1]
+    group = depth * len(gathered)
+    for near, ref in enumerate(gathered):
+        for step in range(steps):
+            part = ref[:, :, step * width : (step + 1) * width]
+            if step < steps - 1:
+                low = step * group + near * depth
+                main_ref[:, low : low + depth, :] = part
+            else:
+                tail_ref[:, near * depth : (near + 1) * depth, :] = part
+
+
+def convolve(ref, main_ref, tail_ref, first, rows):
+    slabs = ref.shape[1] - 2
+    main = main_ref.shape[1]
+    group = tail_ref.shape[1]
+    total = None
+    for tap in range(TAPS):
+        part = jnp.dot(
+            window(ref, first, rows, slabs, tap, 0, main),
+            main_ref[tap],
+            preferred_element_type=F32,
+        )
+        total = part if total is None else total + part
+    tail = tail_ref[...].reshape(TAPS * group, tail_ref.shape[2])
+    return total + jnp.dot(
+        tails(ref, first, rows, slabs, main, group), tail, preferred_element_type=F32
+    )
+
+
+def middle_body(
+    steps, span, act_ref, a_ref, b_ref, c_ref, d_ref, norm_ref, out_ref, main_ref, tail_ref
+):
+    height = act_ref.shape[0] - 2
+    slabs = act_ref.shape[1] - 2
+    width = main_ref.shape[2]
+    place_weights((a_ref, b_ref, c_ref, d_ref), main_ref, tail_ref, steps, width)
+    select = selection(steps, span, 4, out_ref.shape[3] // 128 * 2, width)
+    edge = jnp.zeros(out_ref.shape[1:], BF16)
+    out_ref[0] = edge
+    out_ref[height + 1] = edge
+    hidden = convolve(act_ref, main_ref, tail_ref, 0, height) + norm_ref[4:5, :]
+    value = ((hidden - norm_ref[0:1, :]) * norm_ref[1:2, :]) * norm_ref[2:3, :] + norm_ref[3:4, :]
+    active = silu(value).astype(BF16)
+    ordered = jnp.dot(active, select, preferred_element_type=F32)
+    ordered = ordered.reshape(height, slabs, SLAB, select.shape[1])
+    for row in range(height):
+        store_slabs(out_ref, row + 1, ordered[row])
+
+
+def last_body(
+    steps, act_ref, a_ref, b_ref, c_ref, d_ref, bias_ref, mine_ref,
+    send_ref, keep_ref, main_ref, tail_ref, turned_ref,
+):
+    half = lax.axis_index("rows")
+    local, channels, columns = mine_ref.shape
+    slabs = columns // SLAB
+    width = main_ref.shape[2]
+    place_weights((a_ref, b_ref, c_ref, d_ref), main_ref, tail_ref, steps, width)
+    for keep in (False, True):
+        first = (half if keep else 1 - half) * local
+        part = convolve(act_ref, main_ref, tail_ref, first, local)
+        if keep:
+            part = part + bias_ref[...]
+        padding = jnp.zeros((part.shape[0], -channels % 128), F32)
+        part = jnp.concatenate([part, padding], axis=1).reshape(local, slabs, SLAB, -1)
+        for row in range(local):
+            for tile in range(turned_ref.shape[0]):
+                for slab in range(slabs):
+                    turned_ref[tile, pl.ds(slab, SLAB, stride=slabs), :] = part[
+                        row, slab, :, tile * 128 : (tile + 1) * 128
+                    ]
+            turned = jnp.concatenate(
+                [turned_ref[tile].T for tile in range(turned_ref.shape[0])], axis=0
+            )[:channels]
+            if keep:
+                keep_ref[row] = turned + mine_ref[row].astype(F32)
+            else:
+                send_ref[row] = turned.astype(BF16)
+
+
+def finish_body(keep_ref, got_ref, out_ref):
+    out_ref[...] = (keep_ref[...] + got_ref[...].astype(F32)).astype(BF16)
+
+
+def paired(
+    latents,
+    mean_one,
+    rstd_one,
+    gain_one,
+    shift_one,
+    kernel_one,
+    bias_one,
+    embed_bias,
+    mean_two,
+    rstd_two,
+    gain_two,
+    shift_two,
+    kernel_two,
+    bias_two,
+):
+    channels = latents.shape[3]
+    local, columns = latents.shape[1], latents.shape[2]
+    blocks, taps, length = kernel_one.shape
+    steps = length // channels
+    span = channels // blocks
+    width = channels // 2
+    slabs = columns // SLAB
+    height = 2 * local
+    devices = lax.axis_size("dp")
+    half = lax.axis_index("rows")
+    group_size = channels // mean_one.shape[1]
+    array = jax.ShapeDtypeStruct
+
+    def swap(value, mask):
+        return lax.ppermute(value, "dp", [(i, i ^ mask) for i in range(devices)])
+
+    def across(value):
+        return lax.ppermute(value, "rows", [(0, 1), (1, 0)])
+
+    def spread(groups):
+        return jnp.repeat(groups[0], group_size)
+
+    first, second = call(
+        functools.partial(prepare_body, width),
+        (
+            array((taps, blocks, steps * width), BF16),
+            array((taps, blocks // 2, length), BF16),
+        ),
+        500_000,
+    )(jnp.transpose(kernel_one, (1, 0, 2)), jnp.transpose(kernel_two, (1, 0, 2)))
+
+    mine = jnp.transpose(latents[0], (0, 2, 1))
+    far = [devices // 4, devices // 2, 3 * devices // 4]
+    first_far = [swap(first, mask) for mask in far]
+    other = across(mine)
+    second_far = [swap(second, mask) for mask in far]
+
+    norm_one = jnp.stack([spread(mean_one), spread(rstd_one), gain_one, shift_one])
+    norm_two = jnp.stack(
+        [spread(mean_two), spread(rstd_two), gain_two, shift_two, bias_one + embed_bias[0]]
+    )
+    norm_two = lax.dynamic_slice_in_dim(norm_two, half * width, width, axis=1)
+
+    def widen(near, parts):
+        depth, lanes = near.shape[1:]
+        merged = call(merge_body, array((taps, 4 * depth, lanes), BF16), 1_000_000)(near, *parts)
+        beside = swap(merged, 2)
+        return (merged, beside, swap(merged, 1), swap(beside, 1))
+
+    act = call(
+        functools.partial(first_body, steps, span),
+        array((height + 2, slabs + 2, SLAB, 4 * 4 * blocks * (steps + 1)), BF16),
+        3_000_000,
+        scratch=[pltpu.VMEM((-(-channels // 128), columns, 128), F32)],
+    )(mine, other, norm_one)
+    first_all = widen(first, first_far)
+    second_all = widen(second, second_far)
+    group = 16 * blocks
+    act = call(
+        functools.partial(middle_body, steps, span),
+        array((height + 2, slabs + 2, SLAB, (group // 2) * (steps - 1) + 128), BF16),
+        5_000_000,
+        flops=2 * height * columns * taps * channels * width,
+        scratch=[
+            pltpu.VMEM((taps, group * (steps - 1), width), BF16),
+            pltpu.VMEM((taps, group, width), BF16),
+        ],
+    )(act, *first_all, norm_two)
+    group = group // 2
+    send, keep = call(
+        functools.partial(last_body, steps),
+        (array(mine.shape, BF16), array(mine.shape, F32)),
+        5_000_000,
+        flops=2 * height * columns * taps * channels * width,
+        scratch=[
+            pltpu.VMEM((taps, group * (steps - 1), channels), BF16),
+            pltpu.VMEM((taps, group, channels), BF16),
+            pltpu.VMEM((-(-channels // 128), columns, 128), F32),
+        ],
+    )(act, *second_all, bias_two[None], mine)
+    result = call(finish_body, array(mine.shape, BF16), 1_000_000)(keep, across(send))
+    return jnp.transpose(result, (0, 2, 1))[None]
+
+
+def fits(mesh):
+    return mesh.shape["dp"] == 16 and mesh.shape["rows"] == 2
+
+
 def solution(mesh):
     placed = (
         P("dp", "rows", None, None),
@@ -135,5 +458,6 @@
         P(),
     )
     return jax.shard_map(
-        shards, mesh=mesh, in_specs=placed, out_specs=P("dp", "rows", None, None), check_vma=False
-    )
+        paired if fits(mesh) else shards,
+        mesh=mesh, in_specs=placed, out_specs=P("dp", "rows", None, None), check_vma=False
+    )

time: 97 us -> 43.7 us (0.45)
  the two profiles are of different devices: /device:TPU:0 before, /device:TPU:16 now
where the time goes in v2:
time: 43.7 us; the launch traced here: 43.4 us
  waiting for transfers between devices  16.1 us (37%)
  starting transfers between devices  13.2 us (30%)
  local copies, waits for them, and re-layouts  9.09 us (21%)
  Pallas kernels  4.72 us (11%)
    ppermute x12, starting transfers between devices, swap(): return lax.ppermute(value, 'dp', [(i, i ^ mask) for i in range(devices)])  11 us
    ppermute x12, waiting for transfers between devices, swap(): return lax.ppermute(value, 'dp', [(i, i ^ mask) for i in range(devices)])  10.5 us
    unnamed x28, local copies, waits for them, and re-layouts  8.28 us
    ppermute x2, waiting for transfers between devices, across(): return lax.ppermute(value, 'rows', [(0, 1), (1, 0)])  5.62 us
    ppermute x2, starting transfers between devices, across(): return lax.ppermute(value, 'rows', [(0, 1), (1, 0)])  2.27 us
    pallas_call x1, Pallas kernels, paired(): call(functools.partial(last_body, steps), (array(mine.shape, BF16), array...  1.55 us
    pallas_call x1, Pallas kernels, paired(): call(functools.partial(middle_body, steps, span), array((height + 2, slab...  1.46 us
  transfers between devices with their start and end apart: 14, of which 3 were waited for; matrix products, arithmetic and copies ran while one was open for 2% of the time, Pallas kernels for 5%

profile of v2, /device:TPU:16, one launch (start us, length us, event | category | flops | bytes accessed | tf_op | source)
XLA Modules:
  0.0 43.4 jit_solution(16190206045957423624)
XLA Ops:
  0.0 0.0 copy-start.1
  0.0 0.9 %copy-done.1 = bf16[4,9,1600]{2,0,1:T(4,128)(2,1)S(1)} copy-done((bf16[4,9,1600]{2,0,1:T(4,128)(2,1)S(1)}, bf16[4,9,1600]{2,0,1:T(4,128)(2,1)}, u32[]{:S(2)}) %copy-start.1) | copy-done | bytes 115224
  0.9 0.0 copy-start.2
  0.9 0.9 %copy-done.2 = bf16[4,9,1600]{2,0,1:T(4,128)(2,1)S(1)} copy-done((bf16[4,9,1600]{2,0,1:T(4,128)(2,1)S(1)}, bf16[4,9,1600]{2,0,1:T(4,128)(2,1)}, u32[]{:S(2)}) %copy-start.2) | copy-done | bytes 115224
  1.8 0.1 shard_map.137
  1.9 1.6 %collective-permute-start.1 = (bf16[9,4,800]{2,1,0:T(4,128)(2,1)S(1)}, bf16[9,4,800]{2,1,0:T(4,128)(2,1)S(1)}, u32[]{:S(2)}, u32[]{:S(2)}) collective-permute-start(bf16[9,4,800]{2,1,0:T(4,128)(2,1)S(1)} %get-tuple-element.9.refs_0_), channel_id=1, source_target_pairs={{0,8},{2,10},{4,12},{6,14},{8,0},{10,2},{12,4},{14,6},{16,24},{18,... | collective-permute-start | bytes 172808 | tf_op jit(solution)/shard_map/ppermute | solution.py:369
  3.5 0.3 collective-permute-start.2
  3.9 1.6 %collective-permute-start.3 = (bf16[9,4,800]{2,1,0:T(4,128)(2,1)S(1)}, bf16[9,4,800]{2,1,0:T(4,128)(2,1)S(1)}, u32[]{:S(2)}, u32[]{:S(2)}) collective-permute-start(bf16[9,4,800]{2,1,0:T(4,128)(2,1)S(1)} %get-tuple-element.9.refs_0_), channel_id=1, source_target_pairs={{0,24},{2,26},{4,28},{6,30},{8,16},{10,18},{12,20},{14,22},{16,8},... | collective-permute-start | bytes 172808 | tf_op jit(solution)/shard_map/ppermute | solution.py:369
  5.5 2.5 %collective-permute-start.7 = (bf16[9,2,1600]{2,1,0:T(2,128)(2,1)S(1)}, bf16[9,2,1600]{2,1,0:T(2,128)(2,1)S(1)}, u32[]{:S(2)}, u32[]{:S(2)}) collective-permute-start(bf16[9,2,1600]{2,1,0:T(2,128)(2,1)S(1)} %get-tuple-element.10.refs_0_), channel_id=1, source_target_pairs={{0,8},{2,10},{4,12},{6,14},{8,0},{10,2},{12,4},{14,6},{16,24},{18,... | collective-permute-start | bytes 172808 | tf_op jit(solution)/shard_map/ppermute | solution.py:369
  7.9 0.0 collective-permute-start.8
  7.9 0.0 collective-permute-done.1.refs_1_
  7.9 1.5 %collective-permute-start.9 = (bf16[9,2,1600]{2,1,0:T(2,128)(2,1)S(1)}, bf16[9,2,1600]{2,1,0:T(2,128)(2,1)S(1)}, u32[]{:S(2)}, u32[]{:S(2)}) collective-permute-start(bf16[9,2,1600]{2,1,0:T(2,128)(2,1)S(1)} %get-tuple-element.10.refs_0_), channel_id=1, source_target_pairs={{0,24},{2,26},{4,28},{6,30},{8,16},{10,18},{12,20},{14,22},{16,8},... | collective-permute-start | bytes 172808 | tf_op jit(solution)/shard_map/ppermute | solution.py:369
  9.4 0.0 collective-permute-done.2.refs_2_
  9.4 5.4 %collective-permute-done.3.refs_3_ = bf16[9,4,800]{2,1,0:T(4,128)(2,1)S(1)} collective-permute-done((bf16[9,4,800]{2,1,0:T(4,128)(2,1)S(1)}, bf16[9,4,800]{2,1,0:T(4,128)(2,1)S(1)}, u32[]{:S(2)}, u32[]{:S(2)}) %collective-permute-start.3) | collective-permute-done | bytes 57632 | tf_op jit(solution)/shard_map/ppermute | solution.py:369
  14.8 0.1 shard_map.138.a_ref
  14.9 0.0 copy-start
  14.9 1.6 %collective-permute-start.4 = (bf16[9,16,800]{2,1,0:T(8,128)(2,1)S(1)}, bf16[9,16,800]{2,1,0:T(8,128)(2,1)S(1)}, u32[]{:S(2)}, u32[]{:S(2)}) collective-permute-start(bf16[9,16,800]{2,1,0:T(8,128)(2,1)S(1)} %shard_map.138.a_ref), channel_id=1, source_target_pairs={{0,4},{2,6},{4,0},{6,2},{8,12},{10,14},{12,8},{14,10},{16,20},{18,... | collective-permute-start | bytes 691208 | tf_op jit(solution)/shard_map/ppermute | solution.py:369
  16.4 0.0 collective-permute-done.7.refs_1_
  16.5 0.0 collective-permute-done.8.refs_2_
  16.5 0.0 collective-permute-done.9.refs_3_
  16.5 0.1 shard_map.140.a_ref
  16.6 1.4 %collective-permute-start.10 = (bf16[9,8,1600]{2,1,0:T(8,128)(2,1)S(1)}, bf16[9,8,1600]{2,1,0:T(8,128)(2,1)S(1)}, u32[]{:S(2)}, u32[]{:S(2)}) collective-permute-start(bf16[9,8,1600]{2,1,0:T(8,128)(2,1)S(1)} %shard_map.140.a_ref), channel_id=1, source_target_pairs={{0,4},{2,6},{4,0},{6,2},{8,12},{10,14},{12,8},{14,10},{16,20},{18,... | collective-permute-start | bytes 691208 | tf_op jit(solution)/shard_map/ppermute | solution.py:369
  18.0 0.0 collective-permute-start.5
  18.0 5.1 %collective-permute-done.4.b_ref = bf16[9,16,800]{2,1,0:T(8,128)(2,1)S(1)} collective-permute-done((bf16[9,16,800]{2,1,0:T(8,128)(2,1)S(1)}, bf16[9,16,800]{2,1,0:T(8,128)(2,1)S(1)}, u32[]{:S(2)}, u32[]{:S(2)}) %collective-permute-start.4) | collective-permute-done | bytes 230432 | tf_op jit(solution)/shard_map/ppermute | solution.py:369
  23.1 0.0 collective-permute-start.6
  23.1 0.0 copy-done
  23.1 1.6 %collective-permute-start = (bf16[2,320,128]{2,1,0:T(8,128)(2,1)S(1)}, bf16[2,320,128]{2,1,0:T(8,128)(2,1)S(1)}, u32[]{:S(2)}, u32[]{:S(2)}) collective-permute-start(bf16[2,320,128]{2,1,0:T(8,128)(2,1)S(1)} %bitcast.12), channel_id=1, source_target_pairs={{0,1},{1,0},{2,3},{3,2},{4,5},{5,4},{6,7},{7,6},{8,9},{9,8},{10,11... | collective-permute-start | bytes 491528 | tf_op jit(solution)/shard_map/ppermute | solution.py:372
  24.6 0.0 copy-done.10
  24.6 0.1 broadcast_in_dim.18
  24.7 0.1 stack_reshape.12
  24.8 0.0 copy-start.11
  24.8 0.6 %copy-done.11 = f32[1,32]{1,0:T(1,128)S(1)} copy-done((f32[1,32]{1,0:T(1,128)S(1)}, f32[1,32]{1,0:T(1,128)}, u32[]{:S(2)}) %copy-start.11) | copy-done | bytes 152
  25.5 0.1 broadcast_in_dim.19
  25.6 0.1 stack_reshape.13
  25.7 0.6 %copy-done.4 = f32[320]{0:T(512)S(1)} copy-done((f32[320]{0:T(512)S(1)}, f32[320]{0:T(512)}, u32[]{:S(2)}) %copy-start.4) | copy-done | bytes 1304
  26.2 0.7 %copy-done.5 = f32[320]{0:T(512)S(1)} copy-done((f32[320]{0:T(512)S(1)}, f32[320]{0:T(512)}, u32[]{:S(2)}) %copy-start.5) | copy-done | bytes 1304
  26.9 0.2 collective-permute-start.11
  27.1 0.0 collective-permute-done.10.b_ref
  27.1 0.4 collective-permute-start.12
  27.5 0.0 copy-start.12
  27.5 0.6 %copy-done.12 = f32[1,32]{1,0:T(1,128)S(1)} copy-done((f32[1,32]{1,0:T(1,128)S(1)}, f32[1,32]{1,0:T(1,128)}, u32[]{:S(2)}) %copy-start.12) | copy-done | bytes 152
  28.1 0.1 broadcast_in_dim.20
  28.2 0.1 stack_reshape.14
  28.3 0.0 copy-start.13
  28.3 0.6 %copy-done.13 = f32[1,32]{1,0:T(1,128)S(1)} copy-done((f32[1,32]{1,0:T(1,128)S(1)}, f32[1,32]{1,0:T(1,128)}, u32[]{:S(2)}) %copy-start.13) | copy-done | bytes 152
  29.0 0.1 broadcast_in_dim.21
  29.0 0.1 stack_reshape.15
  29.1 0.6 %copy-done.9 = f32[1,320]{1,0:T(1,128)S(1)} copy-done((f32[1,320]{1,0:T(1,128)S(1)}, f32[1,320]{1,0:T(1,128)}, u32[]{:S(2)}) %copy-start.9) | copy-done | bytes 1304
  29.7 0.7 %copy-done.3 = f32[320]{0:T(512)S(1)} copy-done((f32[320]{0:T(512)S(1)}, f32[320]{0:T(512)}, u32[]{:S(2)}) %copy-start.3) | copy-done | bytes 1304
  30.4 0.7 %copy-done.6 = f32[320]{0:T(512)S(1)} copy-done((f32[320]{0:T(512)S(1)}, f32[320]{0:T(512)}, u32[]{:S(2)}) %copy-start.6) | copy-done | bytes 1304
  31.1 0.7 %copy-done.7 = f32[320]{0:T(512)S(1)} copy-done((f32[320]{0:T(512)S(1)}, f32[320]{0:T(512)}, u32[]{:S(2)}) %copy-start.7) | copy-done | bytes 1304
  31.8 0.7 %copy-done.8 = f32[320]{0:T(512)S(1)} copy-done((f32[320]{0:T(512)S(1)}, f32[320]{0:T(512)}, u32[]{:S(2)}) %copy-start.8) | copy-done | bytes 1304
  32.5 0.1 constant_dynamic-slice_fusion.norm_ref
  32.5 0.0 collective-permute-done.other_ref
  32.5 0.7 %shard_map.136.act_ref = bf16[6,10,16,384]{3,2,1,0:T(8,128)(2,1)S(1)} custom-call(bf16[2,320,128]{2,1,0:T(8,128)(2,1)S(1)} %bitcast.13, bf16[2,320,128]{2,1,0:T(8,128)(2,1)S(1)} %collective-permute-done.other_ref, f32[4,320]{1,0:T(4,128)S(1)} %pad_maximum_fusion.norm_ref), custom_call_target="tpu_custom_call" | custom-call | bytes 3000000 | tf_op jit(solution)/shard_map/pallas_call | solution.py:404
  33.3 0.0 collective-permute-done.5.c_ref
  33.3 0.0 collective-permute-done.6.d_ref
  33.3 1.5 %shard_map.139.act_ref = bf16[6,10,16,256]{3,2,1,0:T(8,128)(2,1)S(1)} custom-call(bf16[6,10,16,384]{3,2,1,0:T(8,128)(2,1)S(1)} %shard_map.136.act_ref, bf16[9,16,800]{2,1,0:T(8,128)(2,1)S(1)} %shard_map.138.a_ref, bf16[9,16,800]{2,1,0:T(8,128)(2,1)S(1)} %collective-permute-done.4.b_ref, bf16[9,16,800]{2,1,0:T(8,128)(2,1)S(1)} %collective-permute-done.5.c_ref, ...), custom_call_target="tpu_custom_call" | custom-call | flops 471859200 | bytes 5000000 | tf_op jit(solution)/shard_map/pallas_call | solution.py:413
  34.8 0.0 collective-permute-done.11.c_ref
  34.8 0.0 collective-permute-done.12.d_ref
  34.8 1.5 %shard_map.141 = (bf16[2,320,128]{2,1,0:T(8,128)(2,1)S(1)}, f32[2,320,128]{2,1,0:T(8,128)S(1)}) custom-call(bf16[6,10,16,256]{3,2,1,0:T(8,128)(2,1)S(1)} %shard_map.139.act_ref, bf16[9,8,1600]{2,1,0:T(8,128)(2,1)S(1)} %shard_map.140.a_ref, bf16[9,8,1600]{2,1,0:T(8,128)(2,1)S(1)} %collective-permute-done.10.b_ref, ...), custom_call_target="tpu_custom_call" | custom-call | flops 471859200 | bytes 5000000 | tf_op jit(solution)/shard_map/pallas_call | solution.py:424
  36.3 0.7 %collective-permute-start.13 = (bf16[2,320,128]{2,1,0:T(8,128)(2,1)S(1)}, bf16[2,320,128]{2,1,0:T(8,128)(2,1)S(1)}, u32[]{:S(2)}, u32[]{:S(2)}) collective-permute-start(bf16[2,320,128]{2,1,0:T(8,128)(2,1)S(1)} %get-tuple-element.12), channel_id=1, source_target_pairs={{0,1},{1,0},{2,3},{3,2},{4,5},{5,4},{6,7},{7,6},{8,9},{9,8},{10,11... | collective-permute-start | bytes 491528 | tf_op jit(solution)/shard_map/ppermute | solution.py:372
  37.1 5.6 %collective-permute-done.13.got_ref = bf16[2,320,128]{2,1,0:T(8,128)(2,1)S(1)} collective-permute-done((bf16[2,320,128]{2,1,0:T(8,128)(2,1)S(1)}, bf16[2,320,128]{2,1,0:T(8,128)(2,1)S(1)}, u32[]{:S(2)}, u32[]{:S(2)}) %collective-permute-start.13) | collective-permute-done | bytes 163872 | tf_op jit(solution)/shard_map/ppermute | solution.py:372
  42.7 0.7 %shard_map.142 = bf16[2,320,128]{2,1,0:T(8,128)(2,1)} custom-call(f32[2,320,128]{2,1,0:T(8,128)S(1)} %get-tuple-element.11.keep_ref, bf16[2,320,128]{2,1,0:T(8,128)(2,1)S(1)} %collective-permute-done.13.got_ref), custom_call_target="tpu_custom_call" | custom-call | bytes 1000000 | tf_op jit(solution)/shard_map/pallas_call | solution.py:435
  (18 shorter events, 0.1 us)
Async XLA Ops:
  0.0 0.9 %copy-start.1 = (bf16[4,9,1600]{2,0,1:T(4,128)(2,1)S(1)}, bf16[4,9,1600]{2,0,1:T(4,128)(2,1)}, u32[]{:S(2)}) copy-start(bf16[4,9,1600]{2,0,1:T(4,128)(2,1)} %param.19) | copy-start | bytes 345604
  0.9 0.9 %copy-start.2 = (bf16[4,9,1600]{2,0,1:T(4,128)(2,1)S(1)}, bf16[4,9,1600]{2,0,1:T(4,128)(2,1)}, u32[]{:S(2)}) copy-start(bf16[4,9,1600]{2,0,1:T(4,128)(2,1)} %param.26) | copy-start | bytes 345604
  1.9 6.0 %collective-permute-start.1 = (bf16[9,4,800]{2,1,0:T(4,128)(2,1)S(1)}, bf16[9,4,800]{2,1,0:T(4,128)(2,1)S(1)}, u32[]{:S(2)}, u32[]{:S(2)}) collective-permute-start(bf16[9,4,800]{2,1,0:T(4,128)(2,1)S(1)} %get-tuple-element.9.refs_0_), channel_id=1, source_target_pairs={{0,8},{2,10},{4,12},{6,14},{8,0},{10,2},{12,4},{14,6},{16,24},{18,... | collective-permute-start | bytes 172808 | tf_op jit(solution)/shard_map/ppermute | solution.py:369
  3.5 5.9 %collective-permute-start.2 = (bf16[9,4,800]{2,1,0:T(4,128)(2,1)S(1)}, bf16[9,4,800]{2,1,0:T(4,128)(2,1)S(1)}, u32[]{:S(2)}, u32[]{:S(2)}) collective-permute-start(bf16[9,4,800]{2,1,0:T(4,128)(2,1)S(1)} %get-tuple-element.9.refs_0_), channel_id=1, source_target_pairs={{0,16},{2,18},{4,20},{6,22},{8,24},{10,26},{12,28},{14,30},{16,0},... | collective-permute-start | bytes 172808 | tf_op jit(solution)/shard_map/ppermute | solution.py:369
  3.9 10.9 %collective-permute-start.3 = (bf16[9,4,800]{2,1,0:T(4,128)(2,1)S(1)}, bf16[9,4,800]{2,1,0:T(4,128)(2,1)S(1)}, u32[]{:S(2)}, u32[]{:S(2)}) collective-permute-start(bf16[9,4,800]{2,1,0:T(4,128)(2,1)S(1)} %get-tuple-element.9.refs_0_), channel_id=1, source_target_pairs={{0,24},{2,26},{4,28},{6,30},{8,16},{10,18},{12,20},{14,22},{16,8},... | collective-permute-start | bytes 172808 | tf_op jit(solution)/shard_map/ppermute | solution.py:369
  5.5 11.0 %collective-permute-start.7 = (bf16[9,2,1600]{2,1,0:T(2,128)(2,1)S(1)}, bf16[9,2,1600]{2,1,0:T(2,128)(2,1)S(1)}, u32[]{:S(2)}, u32[]{:S(2)}) collective-permute-start(bf16[9,2,1600]{2,1,0:T(2,128)(2,1)S(1)} %get-tuple-element.10.refs_0_), channel_id=1, source_target_pairs={{0,8},{2,10},{4,12},{6,14},{8,0},{10,2},{12,4},{14,6},{16,24},{18,... | collective-permute-start | bytes 172808 | tf_op jit(solution)/shard_map/ppermute | solution.py:369
  7.9 8.5 %collective-permute-start.8 = (bf16[9,2,1600]{2,1,0:T(2,128)(2,1)S(1)}, bf16[9,2,1600]{2,1,0:T(2,128)(2,1)S(1)}, u32[]{:S(2)}, u32[]{:S(2)}) collective-permute-start(bf16[9,2,1600]{2,1,0:T(2,128)(2,1)S(1)} %get-tuple-element.10.refs_0_), channel_id=1, source_target_pairs={{0,16},{2,18},{4,20},{6,22},{8,24},{10,26},{12,28},{14,30},{16,0},... | collective-permute-start | bytes 172808 | tf_op jit(solution)/shard_map/ppermute | solution.py:369
  7.9 8.5 %collective-permute-start.9 = (bf16[9,2,1600]{2,1,0:T(2,128)(2,1)S(1)}, bf16[9,2,1600]{2,1,0:T(2,128)(2,1)S(1)}, u32[]{:S(2)}, u32[]{:S(2)}) collective-permute-start(bf16[9,2,1600]{2,1,0:T(2,128)(2,1)S(1)} %get-tuple-element.10.refs_0_), channel_id=1, source_target_pairs={{0,24},{2,26},{4,28},{6,30},{8,16},{10,18},{12,20},{14,22},{16,8},... | collective-permute-start | bytes 172808 | tf_op jit(solution)/shard_map/ppermute | solution.py:369
  14.9 8.2 %copy-start = (bf16[1,2,128,320]{2,3,1,0:T(8,128)(2,1)S(1)}, bf16[1,2,128,320]{2,3,1,0:T(8,128)(2,1)}, u32[]{:S(2)}) copy-start(bf16[1,2,128,320]{2,3,1,0:T(8,128)(2,1)} %param.14) | copy-start | bytes 491524
  14.9 8.2 %collective-permute-start.4 = (bf16[9,16,800]{2,1,0:T(8,128)(2,1)S(1)}, bf16[9,16,800]{2,1,0:T(8,128)(2,1)S(1)}, u32[]{:S(2)}, u32[]{:S(2)}) collective-permute-start(bf16[9,16,800]{2,1,0:T(8,128)(2,1)S(1)} %shard_map.138.a_ref), channel_id=1, source_target_pairs={{0,4},{2,6},{4,0},{6,2},{8,12},{10,14},{12,8},{14,10},{16,20},{18,... | collective-permute-start | bytes 691208 | tf_op jit(solution)/shard_map/ppermute | solution.py:369
  16.6 10.5 %collective-permute-start.10 = (bf16[9,8,1600]{2,1,0:T(8,128)(2,1)S(1)}, bf16[9,8,1600]{2,1,0:T(8,128)(2,1)S(1)}, u32[]{:S(2)}, u32[]{:S(2)}) collective-permute-start(bf16[9,8,1600]{2,1,0:T(8,128)(2,1)S(1)} %shard_map.140.a_ref), channel_id=1, source_target_pairs={{0,4},{2,6},{4,0},{6,2},{8,12},{10,14},{12,8},{14,10},{16,20},{18,... | collective-permute-start | bytes 691208 | tf_op jit(solution)/shard_map/ppermute | solution.py:369
  18.0 15.3 %collective-permute-start.5 = (bf16[9,16,800]{2,1,0:T(8,128)(2,1)S(1)}, bf16[9,16,800]{2,1,0:T(8,128)(2,1)S(1)}, u32[]{:S(2)}, u32[]{:S(2)}) collective-permute-start(bf16[9,16,800]{2,1,0:T(8,128)(2,1)S(1)} %shard_map.138.a_ref), channel_id=1, source_target_pairs={{0,2},{2,0},{4,6},{6,4},{8,10},{10,8},{12,14},{14,12},{16,18},{18,... | collective-permute-start | bytes 691208 | tf_op jit(solution)/shard_map/ppermute | solution.py:369
  23.1 10.2 %collective-permute-start.6 = (bf16[9,16,800]{2,1,0:T(8,128)(2,1)S(1)}, bf16[9,16,800]{2,1,0:T(8,128)(2,1)S(1)}, u32[]{:S(2)}, u32[]{:S(2)}) collective-permute-start(bf16[9,16,800]{2,1,0:T(8,128)(2,1)S(1)} %collective-permute-done.4.b_ref), channel_id=1, source_target_pairs={{0,2},{2,0},{4,6},{6,4},{8,10},{10,8},{12,14},{14,12},{16,18},{18,... | collective-permute-start | bytes 691208 | tf_op jit(solution)/shard_map/ppermute | solution.py:369
  23.1 1.6 %copy-start.10 = (f32[1,32]{1,0:T(1,128)S(1)}, f32[1,32]{1,0:T(1,128)}, u32[]{:S(2)}) copy-start(f32[1,32]{1,0:T(1,128)} %param.15) | copy-start | bytes 388
  23.1 9.5 %collective-permute-start = (bf16[2,320,128]{2,1,0:T(8,128)(2,1)S(1)}, bf16[2,320,128]{2,1,0:T(8,128)(2,1)S(1)}, u32[]{:S(2)}, u32[]{:S(2)}) collective-permute-start(bf16[2,320,128]{2,1,0:T(8,128)(2,1)S(1)} %bitcast.12), channel_id=1, source_target_pairs={{0,1},{1,0},{2,3},{3,2},{4,5},{5,4},{6,7},{7,6},{8,9},{9,8},{10,11... | collective-permute-start | bytes 491528 | tf_op jit(solution)/shard_map/ppermute | solution.py:372
  24.8 0.7 %copy-start.11 = (f32[1,32]{1,0:T(1,128)S(1)}, f32[1,32]{1,0:T(1,128)}, u32[]{:S(2)}) copy-start(f32[1,32]{1,0:T(1,128)} %param.16) | copy-start | bytes 388
  25.6 0.7 %copy-start.4 = (f32[320]{0:T(512)S(1)}, f32[320]{0:T(512)}, u32[]{:S(2)}) copy-start(f32[320]{0:T(512)} %param.17) | copy-start | bytes 3844
  26.2 0.7 %copy-start.5 = (f32[320]{0:T(512)S(1)}, f32[320]{0:T(512)}, u32[]{:S(2)}) copy-start(f32[320]{0:T(512)} %param.18) | copy-start | bytes 3844
  26.9 7.8 %collective-permute-start.11 = (bf16[9,8,1600]{2,1,0:T(8,128)(2,1)S(1)}, bf16[9,8,1600]{2,1,0:T(8,128)(2,1)S(1)}, u32[]{:S(2)}, u32[]{:S(2)}) collective-permute-start(bf16[9,8,1600]{2,1,0:T(8,128)(2,1)S(1)} %shard_map.140.a_ref), channel_id=1, source_target_pairs={{0,2},{2,0},{4,6},{6,4},{8,10},{10,8},{12,14},{14,12},{16,18},{18,... | collective-permute-start | bytes 691208 | tf_op jit(solution)/shard_map/ppermute | solution.py:369
  27.1 7.7 %collective-permute-start.12 = (bf16[9,8,1600]{2,1,0:T(8,128)(2,1)S(1)}, bf16[9,8,1600]{2,1,0:T(8,128)(2,1)S(1)}, u32[]{:S(2)}, u32[]{:S(2)}) collective-permute-start(bf16[9,8,1600]{2,1,0:T(8,128)(2,1)S(1)} %collective-permute-done.10.b_ref), channel_id=1, source_target_pairs={{0,2},{2,0},{4,6},{6,4},{8,10},{10,8},{12,14},{14,12},{16,18},{18,... | collective-permute-start | bytes 691208 | tf_op jit(solution)/shard_map/ppermute | solution.py:369
  27.5 0.7 %copy-start.12 = (f32[1,32]{1,0:T(1,128)S(1)}, f32[1,32]{1,0:T(1,128)}, u32[]{:S(2)}) copy-start(f32[1,32]{1,0:T(1,128)} %param.22) | copy-start | bytes 388
  28.3 0.7 %copy-start.13 = (f32[1,32]{1,0:T(1,128)S(1)}, f32[1,32]{1,0:T(1,128)}, u32[]{:S(2)}) copy-start(f32[1,32]{1,0:T(1,128)} %param.23) | copy-start | bytes 388
  29.0 0.7 %copy-start.9 = (f32[1,320]{1,0:T(1,128)S(1)}, f32[1,320]{1,0:T(1,128)}, u32[]{:S(2)}) copy-start(f32[1,320]{1,0:T(1,128)} %param.21) | copy-start | bytes 3844
  29.7 0.7 %copy-start.3 = (f32[320]{0:T(512)S(1)}, f32[320]{0:T(512)}, u32[]{:S(2)}) copy-start(f32[320]{0:T(512)} %param.20) | copy-start | bytes 3844
  30.4 0.7 %copy-start.6 = (f32[320]{0:T(512)S(1)}, f32[320]{0:T(512)}, u32[]{:S(2)}) copy-start(f32[320]{0:T(512)} %param.24) | copy-start | bytes 3844
  31.1 0.7 %copy-start.7 = (f32[320]{0:T(512)S(1)}, f32[320]{0:T(512)}, u32[]{:S(2)}) copy-start(f32[320]{0:T(512)} %param.25) | copy-start | bytes 3844
  31.8 0.7 %copy-start.8 = (f32[320]{0:T(512)S(1)}, f32[320]{0:T(512)}, u32[]{:S(2)}) copy-start(f32[320]{0:T(512)} %param.27) | copy-start | bytes 3844
  36.3 6.3 %collective-permute-start.13 = (bf16[2,320,128]{2,1,0:T(8,128)(2,1)S(1)}, bf16[2,320,128]{2,1,0:T(8,128)(2,1)S(1)}, u32[]{:S(2)}, u32[]{:S(2)}) collective-permute-start(bf16[2,320,128]{2,1,0:T(8,128)(2,1)S(1)} %get-tuple-element.12), channel_id=1, source_target_pairs={{0,1},{1,0},{2,3},{3,2},{4,5},{5,4},{6,7},{7,6},{8,9},{9,8},{10,11... | collective-permute-start | bytes 491528 | tf_op jit(solution)/shard_map/ppermute | solution.py:372
